TPU v7x, 32 devices: a whole 2x2x4 slice. The times are simulated.
32 devices in a mesh: tok: 8 (over z, core), voc: 4 (over y, x).
Axes of the slice: x: 2, y: 2, z: 4, core: 2. Of those that a mesh axis runs over, the one named last changes fastest.
Arguments:
- hidden: bfloat16 [4096, 1024], P('tok'), may hold values from -64 to 64
- head_weight: bfloat16 [1024, 16384], P('tok', 'voc'), may hold values from -1 to 1
- target_logits: bfloat16 [4096, 16384], P('tok', 'voc'), may hold values from -320 to 320
- token_ids: int32 [4096], P('tok'), may hold values from 0 to 16383
Outputs:
- loss: float32 [], replicated
- grad_hidden: float32 [4096, 1024], P('tok', 'voc')
- grad_head: float32 [1024, 16384], P('tok', 'voc')
All inputs are finite; a program needn't handle non-finite values.
Results may differ from a plain program's by a relative error of at most 0.015.
Values may be sent and summed in bfloat16 or wider, within the bound.
No kernel may reach another device: no remote copies, remote signals or barrier semaphores. Data moves between devices by JAX's collectives and lax.ppermute only.
A program may use at most 128 MiB of HBM per device.

v0:
```python
import jax
import jax.numpy as jnp
from jax import lax
from jax.sharding import PartitionSpec as P

ce_weight = 0.5


def body(hidden, head_weight, target_logits, token_ids):
    rows = hidden.shape[0]
    share = head_weight.shape[1]
    vocab_start = lax.axis_index("voc") * share
    whole = lax.all_gather(head_weight, "tok", axis=0, tiled=True)
    draft = jnp.dot(hidden, whole, preferred_element_type=jnp.float32)
    target = target_logits.astype(jnp.float32)
    target_max, draft_max = lax.pmax((jnp.max(target, axis=1), jnp.max(draft, axis=1)), "voc")
    target_exp = jnp.exp(target - target_max[:, None])
    draft_exp = jnp.exp(draft - draft_max[:, None])
    target_sum, draft_sum = lax.psum(
        (jnp.sum(target_exp, axis=1), jnp.sum(draft_exp, axis=1)), "voc"
    )
    probs_p = target_exp / target_sum[:, None]
    probs_q = draft_exp / draft_sum[:, None]
    lse_t = target_max + jnp.log(target_sum)
    lse_z = draft_max + jnp.log(draft_sum)
    column = lax.broadcasted_iota(jnp.int32, (rows, share), 1) + vocab_start
    own = (column == token_ids[:, None]).astype(jnp.float32)
    voc_count = lax.axis_size("voc")
    per_token = jnp.sum(probs_p * (target - draft) - ce_weight * own * draft, axis=1)
    per_token = per_token + ((1.0 + ce_weight) * lse_z - lse_t) / voc_count
    total = lax.psum(jnp.sum(per_token), ("tok", "voc"))
    loss = total / (rows * lax.axis_size("tok"))
    slope = ((1.0 + ce_weight) * probs_q - probs_p - ce_weight * own).astype(jnp.bfloat16)
    partial_grad = lax.dot_general(
        slope, whole, (((1,), (1,)), ((), ())), preferred_element_type=jnp.float32
    )
    grad_hidden = lax.psum_scatter(
        partial_grad.astype(jnp.bfloat16), "voc", scatter_dimension=1, tiled=True
    ).astype(jnp.float32)
    grad_head = lax.psum_scatter(
        lax.dot_general(
            hidden, slope, (((0,), (0,)), ((), ())), preferred_element_type=jnp.float32
        ).astype(jnp.bfloat16),
        "tok",
        scatter_dimension=0,
        tiled=True,
    ).astype(jnp.float32)
    return (loss, grad_hidden, grad_head)


def solution(mesh):
    placed = (P("tok", None), P("tok", "voc"), P("tok", "voc"), P("tok"))
    return jax.shard_map(
        body,
        mesh=mesh,
        in_specs=placed,
        out_specs=(P(), P("tok", "voc"), P("tok", "voc")),
        check_vma=False,
    )
```

profile of v0, /device:TPU:0, one launch (start us, length us, event | category | flops | bytes accessed | tf_op | source)
XLA Modules:
  0.0 290.3 jit_solution(11293099033932415413)
XLA Ops:
  7.2 0.0 copy-start
  7.2 0.0 all-gather.2.cloned.1.call-start
  7.2 0.7 all-gather.2.cloned.1.call-update
  7.9 0.0 reduce-scatter.5.cloned.1.call-start
  8.0 2.8 reduce_max.23
  10.8 0.0 copy-start.2
  10.8 83.6 %all-gather.2.cloned.1.call-done = bf16[1024,4096]{1,0:T(8,128)(2,1)} async-done(((bf16[128,4096]{1,0:T(8,128)(2,1)}), bf16[1024,4096]{1,0:T(8,128)(2,1)}) %all-gather.2.cloned.1.call-update) | async-done | bytes 8388624 | tf_op jit(solution)/shard_map/all_gather | solution.py:13
  94.4 0.0 copy-done
  94.4 10.1 %fusion.8 = (f32[512]{0:T(512)S(1)}, f32[512,4096]{1,0:T(8,128)}) fusion(bf16[512,1024]{1,0:T(8,128)(2,1)S(1)} %copy-done, bf16[1024,4096]{1,0:T(8,128)(2,1)} %all-gather.2.cloned.1.call-done), kind=kOutput, calls=%fused_computation.17 | convolution fusion | flops 4297063936 | bytes 17827840 | tf_op jit(solution)/shard_map/dot_general | solution.py:14
  104.5 9.8 %all-reduce = (f32[512]{0:T(512)S(1)}, f32[512]{0:T(512)S(1)}) all-reduce(f32[512]{0:T(512)S(1)} %get-tuple-element.13, bf16[512]{0:T(512)(128)(2,1)S(1)} %reduce_max.23), channel_id=1, replica_groups=mesh['tok'=8,'voc'=4] {'voc'}, use_global_device_ids=true, to_apply=%region_6.0 | all-reduce | flops 1024 | bytes 7168 | tf_op jit(solution)/shard_map/pmax | solution.py:16
  114.3 3.7 %fusion.2 = f32[512]{0:T(512)S(1)} fusion(bf16[512,4096]{1,0:T(8,128)(2,1)} %param.6, f32[512]{0:T(512)S(1)} %get-tuple-element.12), kind=kLoop, calls=%fused_computation.6 | loop fusion | flops 6290944 | bytes 4198400 | tf_op jit(solution)/shard_map/reduce_sum | solution.py:20
  118.0 8.0 %psum.21 = f32[512]{0:T(512)S(1)} all-reduce(f32[512]{0:T(512)S(1)} %fusion.2), channel_id=1, replica_groups=mesh['tok'=8,'voc'=4] {'voc'}, use_global_device_ids=true, to_apply=%region_3.0 | all-reduce | flops 512 | bytes 4096 | tf_op jit(solution)/shard_map/psum | solution.py:19
  126.0 0.0 copy-done.2
  126.0 7.6 %fusion.7 = (f32[512]{0:T(512)S(1)}, f32[512]{0:T(512)S(1)}) fusion(f32[512,4096]{1,0:T(8,128)} %get-tuple-element.14, f32[512]{0:T(512)S(1)} %get-tuple-element.11, s32[512]{0:T(512)S(1)} %copy-done.2, s32[4096]{0:T(1024)S(1)} %iota_add_fusion, f32[512]{0:T(512)S(1)} %psum.21, f32[512]{0:T(512)S(1)} %get-tuple-element.12, bf16[512,4096]{1,0:T(8,128)(2,1)} %param.6), kind=kLoop, calls=%fused_computation.13 | loop fusion | flops 25164800 | bytes 12611584 | tf_op jit(solution)/shard_map/reduce_sum | solution.py:20
  133.6 9.2 %psum.22 = f32[512]{0:T(512)S(1)} all-reduce(f32[512]{0:T(512)S(1)} %get-tuple-element.9), channel_id=1, replica_groups=mesh['tok'=8,'voc'=4] {'voc'}, use_global_device_ids=true, to_apply=%region_8.0 | all-reduce | flops 512 | bytes 4096 | tf_op jit(solution)/shard_map/psum | solution.py:19
  142.7 8.1 %fusion.6 = bf16[512,4096]{1,0:T(8,128)(2,1)S(1)} fusion(f32[512,4096]{1,0:T(8,128)} %get-tuple-element.14, bf16[512,4096]{1,0:T(8,128)(2,1)} %param.6, f32[512]{0:T(512)S(1)} %psum.22, f32[512]{0:T(512)S(1)} %get-tuple-element.11, s32[4096]{0:T(1024)S(1)} %iota_add_fusion, f32[512]{0:T(512)S(1)} %psum.21, f32[512]{0:T(512)S(1)} %get-tuple-element.12, ...), kind=kLoop, calls=%fused_computation.10 | loop fusion | flops 23068672 | bytes 16803840 | tf_op jit(solution)/shard_map/convert_element_type | solution.py:33
  150.8 0.0 copy-start.1
  150.8 2.0 copy-done.1
  152.8 8.0 %convolution_convert_fusion = bf16[512,1024]{1,0:T(8,128)(2,1)} fusion(bf16[512,4096]{1,0:T(8,128)(2,1)S(1)} %fusion.6, bf16[1024,4096]{1,0:T(8,128)(2,1)} %all-gather.2.cloned.1.call-done), kind=kOutput, calls=%fused_computation.14 | convolution fusion | flops 4295491584 | bytes 13631488 | tf_op jit(solution)/shard_map/dot_general | solution.py:34
  160.8 0.0 reduce-scatter.5.cloned.1.call-update
  160.9 0.0 reduce-scatter.7.cloned.1.call-start
  160.9 9.0 %convert_bitcast_fusion = bf16[1024,4096]{0,1:T(8,128)(2,1)} fusion(bf16[512,4096]{1,0:T(8,128)(2,1)} %copy-done.1, bf16[512,1024]{1,0:T(8,128)(2,1)S(1)} %copy-done), kind=kOutput, calls=%fused_computation.11 | convolution fusion | flops 4299161600 | bytes 13631488 | tf_op jit(solution)/shard_map/dot_general | solution.py:41
  169.9 11.3 %copy.9 = bf16[1024,4096]{1,0:T(8,128)(2,1)} copy(bf16[1024,4096]{0,1:T(8,128)(2,1)} %convert_bitcast_fusion) | data formatting | bytes 16777216
  181.3 0.0 reduce-scatter.7.cloned.1.call-update
  181.3 0.6 add_reduce_fusion
  181.9 39.5 %psum.23 = f32[]{:T(128)} all-reduce(f32[]{:T(128)} %add_reduce_fusion), channel_id=1, replica_groups=mesh['tok'=8,'voc'=4] {'tok','voc'}, use_global_device_ids=true, to_apply=%region_10.0 | all-reduce | flops 1 | bytes 8 | tf_op jit(solution)/shard_map/psum | solution.py:31
  222.1 0.0 reduce-scatter.5.cloned.1.call-done
  222.1 1.8 convert_element_type.25
  223.9 55.5 %reduce-scatter.7.cloned.1.call-done = bf16[128,4096]{1,0:T(8,128)(2,1)} async-done(((bf16[1024,4096]{1,0:T(8,128)(2,1)}), bf16[128,4096]{1,0:T(8,128)(2,1)}) %reduce-scatter.7.cloned.1.call-update) | async-done | bytes 1048592
  279.4 1.6 copy.10
  281.0 1.6 copy.8
  (1 shorter events, 0.0 us)
Async XLA Ops:
  7.2 87.2 %copy-start = (bf16[512,1024]{1,0:T(8,128)(2,1)S(1)}, bf16[512,1024]{1,0:T(8,128)(2,1)}, u32[]{:S(2)}) copy-start(bf16[512,1024]{1,0:T(8,128)(2,1)} %param.4) | copy-start | bytes 3145732
  7.2 87.2 %all-gather.2.cloned.1.call-start = ((), (), s32[]{:S(2)}) async-start(), calls=%async_computation.2 | async-start | bytes 9437184 | tf_op jit(solution)/shard_map/all_gather | solution.py:13
  7.9 214.2 %reduce-scatter.5.cloned.1.call-start = ((), (), s32[]{:S(2)}) async-start(), calls=%async_computation.3 | async-start | bytes 1310720 | tf_op jit(solution)/shard_map/reduce_scatter | solution.py:37
  10.8 115.2 %copy-start.2 = (s32[512]{0:T(512)S(1)}, s32[512]{0:T(512)}, u32[]{:S(2)}) copy-start(s32[512]{0:T(512)} %param.7) | copy-start | bytes 6148
  150.8 2.0 copy-start.1
  160.9 118.5 %reduce-scatter.7.cloned.1.call-start = ((), (), s32[]{:S(2)}) async-start(), calls=%async_computation.4 | async-start | bytes 9437184
Sparse Core Ops, SparseCore 0:
  9.6 84.7 all-gather.1
  161.0 25.4 reduce-scatter.4
  188.8 90.5 reduce-scatter.6
where the time goes:
time: 291 us; the launch traced here: 290 us
  waiting for transfers between devices  140 us (48%)
  blocking collectives  66.4 us (23%)
  matrix products  27.2 us (9%)
  other arithmetic  24.6 us (8%)
  local copies, waits for them, and re-layouts  16.5 us (6%)
  between operations  15.6 us (5%)
    all_gather x1, waiting for transfers between devices, body(): whole = lax.all_gather(head_weight, 'tok', axis=0, tiled=True)  83.6 us
    unnamed x4, waiting for transfers between devices  56.3 us
    psum x1, blocking collectives, body(): total = lax.psum(jnp.sum(per_token), ('tok', 'voc'))  39.5 us
    psum x2, blocking collectives, body(): lax.psum((jnp.sum(target_exp, axis=1), jnp.sum(draft_exp, axis=1)), 'voc')  17.1 us
    unnamed x9, local copies, waits for them, and re-layouts  16.5 us
    dot_general x1, matrix products, body(): draft = jnp.dot(hidden, whole, preferred_element_type=jnp.float32)  10.1 us
    pmax x1, blocking collectives, body(): lax.pmax((jnp.max(target, axis=1), jnp.max(draft, axis=1)), 'voc')  9.81 us
    dot_general x1, matrix products, body(): lax.dot_general(hidden, slope, (((0,), (0,)), ((), ())), preferred_elemen...  9.02 us
  transfers between devices with their start and end apart: 3, of which 2 were waited for; matrix products, arithmetic and copies ran while one was open for 9% of the time, Pallas kernels for 0%

commit v1 on v0

--- a/solution.py
+++ b/solution.py
@@ -10,7 +10,14 @@
     rows = hidden.shape[0]
     share = head_weight.shape[1]
     vocab_start = lax.axis_index("voc") * share
-    whole = lax.all_gather(head_weight, "tok", axis=0, tiled=True)
+    x = head_weight
+    ways, here, turn = (lax.axis_size("tok"), lax.axis_index("tok"), x.shape[0])
+    shape = [n * ways if d == 0 else n for d, n in enumerate(x.shape)]
+    full = lax.dynamic_update_slice_in_dim(jnp.zeros(shape, x.dtype), x, here * turn, axis=0)
+    for far in range(1, ways):
+        x = lax.ppermute(x, "tok", [(d, (d + 1) % ways) for d in range(ways)])
+        full = lax.dynamic_update_slice_in_dim(full, x, (here - far) % ways * turn, axis=0)
+    whole = full
     draft = jnp.dot(hidden, whole, preferred_element_type=jnp.float32)
     target = target_logits.astype(jnp.float32)
     target_max, draft_max = lax.pmax((jnp.max(target, axis=1), jnp.max(draft, axis=1)), "voc")

time: 291 us -> 316 us (1.086)
  waiting for transfers between devices: 140 us -> 156 us
  local copies, waits for them, and re-layouts: 16.5 us -> 29.4 us
    ppermute x0 -> x7, waiting for transfers between devices: none -> 99.6 us  [body(): x = lax.ppermute(x, 'tok', [(d, (d + 1) % ways) for d in range(ways)])]
    all_gather x1 -> x0, waiting for transfers between devices: 83.6 us -> none  [body(): whole = lax.all_gather(head_weight, 'tok', axis=0, tiled=True)]
    unnamed x9 -> x22, local copies, waits for them, and re-layouts: 16.5 us -> 25 us
    dynamic_update_slice x0 -> x8, local copies, waits for them, and re-layouts: none -> 3.34 us  [the longest x7 3.23 us: body(): lax.dynamic_update_slice_in_dim(full, x, (here - far) % ways * turn, axis=0)]
    unnamed x4 -> x3, waiting for transfers between devices: 56.3 us -> 56.1 us
  transfers between devices with their start and end apart: 3 -> 9, of which waited for: 2 -> 8; matrix products, arithmetic and copies ran while one was open for 9% -> 12% of each run, Pallas kernels for 0% -> 0%
where the time goes in v1:
time: 316 us
  waiting for transfers between devices  156 us (49%)
  blocking collectives  66.2 us (21%)
  local copies, waits for them, and re-layouts  29.4 us (9%)
  matrix products  24.5 us (8%)
  other arithmetic  23.1 us (7%)
  between operations  16.1 us (5%)
    ppermute x7, waiting for transfers between devices, body(): x = lax.ppermute(x, 'tok', [(d, (d + 1) % ways) for d in range(ways)])  99.6 us
    unnamed x3, waiting for transfers between devices  56.1 us
    psum x1, blocking collectives, body(): total = lax.psum(jnp.sum(per_token), ('tok', 'voc'))  38.7 us
    unnamed x22, local copies, waits for them, and re-layouts  25 us
    psum x2, blocking collectives, body(): lax.psum((jnp.sum(target_exp, axis=1), jnp.sum(draft_exp, axis=1)), 'voc')  17.1 us
    pmax x1, blocking collectives, body(): lax.pmax((jnp.max(target, axis=1), jnp.max(draft, axis=1)), 'voc')  10.4 us
    dot_general x1, matrix products, body(): lax.dot_general(hidden, slope, (((0,), (0,)), ((), ())), preferred_elemen...  8.93 us
    dot_general x1, matrix products, body(): lax.dot_general(slope, whole, (((1,), (1,)), ((), ())), preferred_element...  8.21 us
  transfers between devices with their start and end apart: 9, of which 8 were waited for; matrix products, arithmetic and copies ran while one was open for 12% of the time, Pallas kernels for 0%

profile of v1, /device:TPU:0, one launch (start us, length us, event | category | flops | bytes accessed | tf_op | source)
XLA Modules:
  0.0 315.6 jit_solution(1784160881387144635)
XLA Ops:
  7.2 0.5 collective-permute-start
  7.8 16.7 %collective-permute-done = bf16[128,4096]{1,0:T(8,128)(2,1)S(1)} collective-permute-done((bf16[128,4096]{1,0:T(8,128)(2,1)}, bf16[128,4096]{1,0:T(8,128)(2,1)S(1)}, u32[]{:S(2)}, u32[]{:S(2)}) %collective-permute-start) | collective-permute-done | bytes 1048608 | tf_op jit(solution)/shard_map/ppermute | solution.py:18
  24.5 16.0 %collective-permute-done.1 = bf16[128,4096]{1,0:T(8,128)(2,1)S(1)} collective-permute-done((bf16[128,4096]{1,0:T(8,128)(2,1)S(1)}, bf16[128,4096]{1,0:T(8,128)(2,1)S(1)}, u32[]{:S(2)}, u32[]{:S(2)}) %collective-permute-start.1) | collective-permute-done | bytes 1048608 | tf_op jit(solution)/shard_map/ppermute | solution.py:18
  40.5 1.0 copy-done.4
  41.5 16.0 %collective-permute-done.2 = bf16[128,4096]{1,0:T(8,128)(2,1)S(1)} collective-permute-done((bf16[128,4096]{1,0:T(8,128)(2,1)S(1)}, bf16[128,4096]{1,0:T(8,128)(2,1)S(1)}, u32[]{:S(2)}, u32[]{:S(2)}) %collective-permute-start.2) | collective-permute-done | bytes 1048608 | tf_op jit(solution)/shard_map/ppermute | solution.py:18
  57.5 1.0 copy-done.6
  58.5 16.1 %collective-permute-done.3 = bf16[128,4096]{1,0:T(8,128)(2,1)} collective-permute-done((bf16[128,4096]{1,0:T(8,128)(2,1)S(1)}, bf16[128,4096]{1,0:T(8,128)(2,1)}, u32[]{:S(2)}, u32[]{:S(2)}) %collective-permute-start.3) | collective-permute-done | bytes 1048608 | tf_op jit(solution)/shard_map/ppermute | solution.py:18
  74.6 6.5 %copy.9 = bf16[512,4096]{0,1:T(8,128)(2,1)} copy(bf16[512,4096]{1,0:T(8,128)(2,1)} %param.6) | data formatting | bytes 8388608 | tf_op args[2]
  81.1 2.9 reduce_max.23
  84.1 1.0 broadcast_in_dim.2
  85.3 5.7 %collective-permute-done.4 = bf16[128,4096]{1,0:T(8,128)(2,1)} collective-permute-done((bf16[128,4096]{1,0:T(8,128)(2,1)}, bf16[128,4096]{1,0:T(8,128)(2,1)}, u32[]{:S(2)}, u32[]{:S(2)}) %collective-permute-start.4) | collective-permute-done | bytes 1048608 | tf_op jit(solution)/shard_map/ppermute | solution.py:18
  91.3 15.9 %collective-permute-done.5 = bf16[128,4096]{1,0:T(8,128)(2,1)S(1)} collective-permute-done((bf16[128,4096]{1,0:T(8,128)(2,1)}, bf16[128,4096]{1,0:T(8,128)(2,1)S(1)}, u32[]{:S(2)}, u32[]{:S(2)}) %collective-permute-start.5) | collective-permute-done | bytes 1048608 | tf_op jit(solution)/shard_map/ppermute | solution.py:18
  107.2 1.3 constant_dynamic-update-slice_fusion.3
  108.5 1.3 constant_dynamic-update-slice_fusion.2
  110.0 13.2 %collective-permute-done.6 = bf16[128,4096]{1,0:T(8,128)(2,1)S(1)} collective-permute-done((bf16[128,4096]{1,0:T(8,128)(2,1)S(1)}, bf16[128,4096]{1,0:T(8,128)(2,1)S(1)}, u32[]{:S(2)}, u32[]{:S(2)}) %collective-permute-start.6) | collective-permute-done | bytes 1048608 | tf_op jit(solution)/shard_map/ppermute | solution.py:18
  123.4 7.4 %fusion.9 = (f32[512]{0:T(512)S(1)}, f32[4096,512]{1,0:T(8,128)}) fusion(bf16[1024,4096]{1,0:T(8,128)(2,1)S(1)} %constant_dynamic-update-slice_fusion, bf16[512,1024]{1,0:T(8,128)(2,1)S(1)} %copy-done), kind=kOutput, calls=%fused_computation.26 | convolution fusion | flops 4297063936 | bytes 17827840 | tf_op jit(solution)/shard_map/dot_general | solution.py:21
  130.7 10.4 %all-reduce = (f32[512]{0:T(512)S(1)}, f32[512]{0:T(512)S(1)}) all-reduce(f32[512]{0:T(512)S(1)} %get-tuple-element.13, bf16[512]{0:T(512)(128)(2,1)S(1)} %reduce_max.23), channel_id=1, replica_groups=mesh['tok'=8,'voc'=4] {'voc'}, use_global_device_ids=true, to_apply=%region_6.7 | all-reduce | flops 1024 | bytes 7168 | tf_op jit(solution)/shard_map/pmax | solution.py:23
  141.1 3.6 %fusion.2 = f32[512]{0:T(512)S(1)} fusion(bf16[512,4096]{0,1:T(8,128)(2,1)} %copy.9, f32[512]{0:T(512)S(1)} %get-tuple-element.12), kind=kLoop, calls=%fused_computation.6 | loop fusion | flops 6290944 | bytes 4198400 | tf_op jit(solution)/shard_map/reduce_sum | solution.py:27
  144.8 7.9 %psum.21 = f32[512]{0:T(512)S(1)} all-reduce(f32[512]{0:T(512)S(1)} %fusion.2), channel_id=1, replica_groups=mesh['tok'=8,'voc'=4] {'voc'}, use_global_device_ids=true, to_apply=%region_3.4 | all-reduce | flops 512 | bytes 4096 | tf_op jit(solution)/shard_map/psum | solution.py:26
  152.7 7.2 %fusion.8 = (f32[512]{0:T(512)S(1)}, f32[512]{0:T(512)S(1)}) fusion(f32[4096,512]{1,0:T(8,128)} %get-tuple-element.14, f32[512]{0:T(512)S(1)} %get-tuple-element.11, s32[512]{0:T(512)S(1)} %copy-done.8, s32[4096]{0:T(1024)S(1)} %iota_add_fusion, f32[512]{0:T(512)S(1)} %psum.21, f32[512]{0:T(512)S(1)} %get-tuple-element.12, bf16[512,4096]{0,1:T(8,128)(2,1)} %copy.9), kind=kLoop, calls=%fused_computation.14 | loop fusion | flops 25164800 | bytes 12611584 | tf_op jit(solution)/shard_map/reduce_sum | solution.py:27
  159.9 9.2 %psum.22 = f32[512]{0:T(512)S(1)} all-reduce(f32[512]{0:T(512)S(1)} %get-tuple-element.9), channel_id=1, replica_groups=mesh['tok'=8,'voc'=4] {'voc'}, use_global_device_ids=true, to_apply=%region_8.9 | all-reduce | flops 512 | bytes 4096 | tf_op jit(solution)/shard_map/psum | solution.py:26
  169.1 6.9 %fusion.6 = bf16[512,4096]{0,1:T(8,128)(2,1)S(1)} fusion(f32[4096,512]{1,0:T(8,128)} %get-tuple-element.14, bf16[512,4096]{0,1:T(8,128)(2,1)} %copy.9, f32[512]{0:T(512)S(1)} %psum.22, f32[512]{0:T(512)S(1)} %get-tuple-element.11, s32[512]{0:T(512)S(1)} %copy-done.8, f32[512]{0:T(512)S(1)} %psum.21, f32[512]{0:T(512)S(1)} %get-tuple-element.12, ...), kind=kLoop, calls=%fused_computation.10 | loop fusion | flops 23068672 | bytes 16803840 | tf_op jit(solution)/shard_map/convert_element_type | solution.py:40
  176.1 1.9 copy-done.2
  178.0 8.2 %convolution_convert_fusion = bf16[512,1024]{1,0:T(8,128)(2,1)} fusion(bf16[512,4096]{0,1:T(8,128)(2,1)S(1)} %fusion.6, bf16[1024,4096]{1,0:T(8,128)(2,1)} %copy-done.1), kind=kOutput, calls=%fused_computation.15 | convolution fusion | flops 4295491584 | bytes 13631488 | tf_op jit(solution)/shard_map/dot_general | solution.py:41
  186.3 8.9 %convert_bitcast_fusion = bf16[1024,4096]{0,1:T(8,128)(2,1)} fusion(bf16[512,4096]{0,1:T(8,128)(2,1)} %copy-done.2, bf16[512,1024]{1,0:T(8,128)(2,1)S(1)} %copy-done), kind=kOutput, calls=%fused_computation.13 | convolution fusion | flops 4299161600 | bytes 13631488 | tf_op jit(solution)/shard_map/dot_general | solution.py:48
  195.2 11.3 %copy.11 = bf16[1024,4096]{1,0:T(8,128)(2,1)} copy(bf16[1024,4096]{0,1:T(8,128)(2,1)} %convert_bitcast_fusion) | data formatting | bytes 16777216
  206.6 0.6 add_reduce_fusion
  207.2 38.7 %psum.23 = f32[]{:T(128)} all-reduce(f32[]{:T(128)} %add_reduce_fusion), channel_id=1, replica_groups=mesh['tok'=8,'voc'=4] {'tok','voc'}, use_global_device_ids=true, to_apply=%region_10.11 | all-reduce | flops 1 | bytes 8 | tf_op jit(solution)/shard_map/psum | solution.py:38
  246.5 1.8 convert_element_type.25
  248.3 56.1 %reduce-scatter.7.cloned.1.call-done = bf16[128,4096]{1,0:T(8,128)(2,1)} async-done(((bf16[1024,4096]{1,0:T(8,128)(2,1)}), bf16[128,4096]{1,0:T(8,128)(2,1)}) %reduce-scatter.7.cloned.1.call-update) | async-done | bytes 1048592
  304.4 1.6 copy.12
  306.0 1.6 copy.10
  (33 shorter events, 0.9 us)
Async XLA Ops:
  7.2 116.2 %copy-start = (bf16[512,1024]{1,0:T(8,128)(2,1)S(1)}, bf16[512,1024]{1,0:T(8,128)(2,1)}, u32[]{:S(2)}) copy-start(bf16[512,1024]{1,0:T(8,128)(2,1)} %param.4) | copy-start | bytes 3145732
  7.2 239.3 %reduce-scatter.5.cloned.1.call-start = ((), (), s32[]{:S(2)}) async-start(), calls=%async_computation.2 | async-start | bytes 1310720 | tf_op jit(solution)/shard_map/reduce_scatter | solution.py:44
  7.2 17.3 %collective-permute-start = (bf16[128,4096]{1,0:T(8,128)(2,1)}, bf16[128,4096]{1,0:T(8,128)(2,1)S(1)}, u32[]{:S(2)}, u32[]{:S(2)}) collective-permute-start(bf16[128,4096]{1,0:T(8,128)(2,1)} %param.5), channel_id=1, source_target_pairs={{0,4},{4,8},{8,12},{12,16},{16,20},{20,24},{24,28},{28,0},{1,5},{5... | collective-permute-start | bytes 3145736 | tf_op jit(solution)/shard_map/ppermute | solution.py:18
  24.5 16.0 %collective-permute-start.1 = (bf16[128,4096]{1,0:T(8,128)(2,1)S(1)}, bf16[128,4096]{1,0:T(8,128)(2,1)S(1)}, u32[]{:S(2)}, u32[]{:S(2)}) collective-permute-start(bf16[128,4096]{1,0:T(8,128)(2,1)S(1)} %collective-permute-done), channel_id=1, source_target_pairs={{0,4},{4,8},{8,12},{12,16},{16,20},{20,24},{24,28},{28,0},{1,5},{5... | collective-permute-start | bytes 3145736 | tf_op jit(solution)/shard_map/ppermute | solution.py:18
  40.5 1.0 copy-start.4
  41.5 16.0 %collective-permute-start.2 = (bf16[128,4096]{1,0:T(8,128)(2,1)S(1)}, bf16[128,4096]{1,0:T(8,128)(2,1)S(1)}, u32[]{:S(2)}, u32[]{:S(2)}) collective-permute-start(bf16[128,4096]{1,0:T(8,128)(2,1)S(1)} %collective-permute-done.1), channel_id=1, source_target_pairs={{0,4},{4,8},{8,12},{12,16},{16,20},{20,24},{24,28},{28,0},{1,5},{5... | collective-permute-start | bytes 3145736 | tf_op jit(solution)/shard_map/ppermute | solution.py:18
  57.5 1.0 copy-start.6
  58.5 16.1 %collective-permute-start.3 = (bf16[128,4096]{1,0:T(8,128)(2,1)S(1)}, bf16[128,4096]{1,0:T(8,128)(2,1)}, u32[]{:S(2)}, u32[]{:S(2)}) collective-permute-start(bf16[128,4096]{1,0:T(8,128)(2,1)S(1)} %collective-permute-done.2), channel_id=1, source_target_pairs={{0,4},{4,8},{8,12},{12,16},{16,20},{20,24},{24,28},{28,0},{1,5},{5... | collective-permute-start | bytes 3145736 | tf_op jit(solution)/shard_map/ppermute | solution.py:18
  74.6 16.3 %collective-permute-start.4 = (bf16[128,4096]{1,0:T(8,128)(2,1)}, bf16[128,4096]{1,0:T(8,128)(2,1)}, u32[]{:S(2)}, u32[]{:S(2)}) collective-permute-start(bf16[128,4096]{1,0:T(8,128)(2,1)} %collective-permute-done.3), channel_id=1, source_target_pairs={{0,4},{4,8},{8,12},{12,16},{16,20},{20,24},{24,28},{28,0},{1,5},{5... | collective-permute-start | bytes 3145736 | tf_op jit(solution)/shard_map/ppermute | solution.py:18
  81.1 4.0 %copy-start.3 = (bf16[128,4096]{1,0:T(8,128)(2,1)S(1)}, bf16[128,4096]{1,0:T(8,128)(2,1)}, u32[]{:S(2)}) copy-start(bf16[128,4096]{1,0:T(8,128)(2,1)} %param.5) | copy-start | bytes 3145732
  84.1 7.0 %copy-start.5 = (bf16[128,4096]{1,0:T(8,128)(2,1)S(1)}, bf16[128,4096]{1,0:T(8,128)(2,1)}, u32[]{:S(2)}) copy-start(bf16[128,4096]{1,0:T(8,128)(2,1)} %copy-done.4) | copy-start | bytes 3145732
  84.1 7.1 %copy-start.7 = (bf16[128,4096]{1,0:T(8,128)(2,1)S(1)}, bf16[128,4096]{1,0:T(8,128)(2,1)}, u32[]{:S(2)}) copy-start(bf16[128,4096]{1,0:T(8,128)(2,1)} %copy-done.6) | copy-start | bytes 3145732
  91.0 16.2 %collective-permute-start.5 = (bf16[128,4096]{1,0:T(8,128)(2,1)}, bf16[128,4096]{1,0:T(8,128)(2,1)S(1)}, u32[]{:S(2)}, u32[]{:S(2)}) collective-permute-start(bf16[128,4096]{1,0:T(8,128)(2,1)} %collective-permute-done.4), channel_id=1, source_target_pairs={{0,4},{4,8},{8,12},{12,16},{16,20},{20,24},{24,28},{28,0},{1,5},{5... | collective-permute-start | bytes 3145736 | tf_op jit(solution)/shard_map/ppermute | solution.py:18
  107.2 16.0 %collective-permute-start.6 = (bf16[128,4096]{1,0:T(8,128)(2,1)S(1)}, bf16[128,4096]{1,0:T(8,128)(2,1)S(1)}, u32[]{:S(2)}, u32[]{:S(2)}) collective-permute-start(bf16[128,4096]{1,0:T(8,128)(2,1)S(1)} %collective-permute-done.5), channel_id=1, source_target_pairs={{0,4},{4,8},{8,12},{12,16},{16,20},{20,24},{24,28},{28,0},{1,5},{5... | collective-permute-start | bytes 3145736 | tf_op jit(solution)/shard_map/ppermute | solution.py:18
  123.3 7.4 %copy-start.1 = (bf16[1024,4096]{1,0:T(8,128)(2,1)}, bf16[1024,4096]{1,0:T(8,128)(2,1)S(1)}, u32[]{:S(2)}) copy-start(bf16[1024,4096]{1,0:T(8,128)(2,1)S(1)} %constant_dynamic-update-slice_fusion) | copy-start | bytes 25165828
  123.4 29.3 %copy-start.8 = (s32[512]{0:T(512)S(1)}, s32[512]{0:T(512)}, u32[]{:S(2)}) copy-start(s32[512]{0:T(512)} %param.7) | copy-start | bytes 6148
  176.1 1.9 copy-start.2
  186.2 118.2 %reduce-scatter.7.cloned.1.call-start = ((), (), s32[]{:S(2)}) async-start(), calls=%async_computation.3 | async-start | bytes 9437184
Sparse Core Ops, SparseCore 0:
  186.4 25.0 reduce-scatter.4
  213.8 90.5 reduce-scatter.6
